TPU v7x, 512 devices: a whole 4x4x16 slice. The times are simulated.
512 devices in a mesh: ctx: 8 (over y, z_hi), tp: 64 (over x, z_lo, core).
Axes of the slice: x: 4, y: 4, z: 16 (z_hi: 2, z_lo: 8; z = z_hi * 8 + z_lo), core: 2. Of those that a mesh axis runs over, the one named last changes fastest.
Arguments:
- hidden: bfloat16 [2048, 2048], P(('ctx', 'tp')), may hold values from -6 to 6
- w_in: bfloat16 [2048, 8192], P(None, 'tp'), may hold values from -0.125 to 0.125
- w_bc: bfloat16 [2048, 32], replicated, may hold values from -0.125 to 0.125
- w_dt: bfloat16 [64, 2048], P('tp'), may hold values from -0.125 to 0.125
- dt_bias: float32 [64], P('tp'), may hold values from -5 to -3
- a_log: float32 [64], P('tp'), may hold values from -4.6 to 0
- d_skip: float32 [64], P('tp'), may hold values from 0.5 to 1.5
- conv_w: float32 [4, 4096], P(None, 'tp'), may hold values from -3 to 3
- w_out: bfloat16 [4096, 2048], P('tp'), may hold values from -0.09375 to 0.09375
- d_out: bfloat16 [2048, 2048], P(('ctx', 'tp')), may hold values from -6 to 6
Outputs:
- d_hidden: bfloat16 [2048, 2048], P(('ctx', 'tp'))
- d_w_in: float32 [2048, 8192], P(None, 'tp')
- d_w_out: float32 [4096, 2048], P('tp')
- d_w_bc: float32 [2048, 32], replicated
All inputs are finite; a program needn't handle non-finite values.
Results may differ from a plain program's by a relative error of at most 0.017.
Values may be sent and summed in bfloat16 or wider, within the bound.
A program may use at most 64 MiB of HBM per device.

v0:
```python
import math
import jax
import jax.numpy as jnp
from jax import lax
from jax.sharding import PartitionSpec as P

STATE = 16
CONV = 4
precise = lax.Precision.HIGHEST


def padded(array, sides, width):
    for axis, dim in sides:
        size, length = (lax.axis_size(axis), array.shape[dim])
        up = [(i, (i + 1) % size) for i in range(size - 1)]
        down = [(j, i) for i, j in up]
        last = lax.slice_in_dim(array, length - width, length, axis=dim)
        leading = lax.slice_in_dim(array, 0, width, axis=dim)
        before = lax.ppermute(last, axis, up)
        after = lax.ppermute(leading, axis, down)
        array = jnp.concatenate([before, array, after], axis=dim)
    return array


def entering(array, axis, combine, identity, reverse):
    length, index = (lax.axis_size(axis), lax.axis_index(axis))
    everything = jax.tree.map(lambda part: lax.all_gather(part, axis), array)
    start = jax.tree.map(
        lambda part, zero: jnp.broadcast_to(jnp.asarray(zero, part.dtype), part.shape),
        array,
        identity,
    )

    def step(k, before):
        at = length - 1 - k if reverse else k
        reached = at > index if reverse else at < index
        new = combine(before, jax.tree.map(lambda part: part[at], everything))
        return jax.tree.map(lambda a, b: jnp.where(reached, a, b), new, before)

    return lax.fori_loop(0, length, step, start)


def times_rows(operand_a, operand_b):
    return lax.dot_general(
        operand_a, operand_b, (((1,), (1,)), ((), ())), preferred_element_type=jnp.float32
    )


def across_rows(operand_a, operand_b):
    return lax.dot_general(
        operand_a, operand_b, (((0,), (0,)), ((), ())), preferred_element_type=jnp.float32
    )


def conv_silu(x_ext, conv_w):
    length = x_ext.shape[0] - CONV + 1
    summed = conv_w[0] * x_ext[0:length]
    for shift_k in range(1, CONV):
        summed = summed + conv_w[shift_k] * x_ext[shift_k : shift_k + length]
    return jax.nn.silu(summed)


def block_ssd(conv_out, steps_dt, b_rows, c_rows, decay_rate, state_in):
    positions = conv_out.shape[0]
    log_keep = jnp.cumsum(steps_dt * decay_rate)
    causal = lax.broadcasted_iota(jnp.int32, (positions, positions), 0) >= lax.broadcasted_iota(
        jnp.int32, (positions, positions), 1
    )
    decays = jnp.exp(jnp.where(causal, log_keep[:, None] - log_keep[None, :], -jnp.inf))
    scores = jnp.einsum("in,jn->ij", c_rows, b_rows, precision=precise) * decays
    weighted = steps_dt[:, None] * conv_out
    outputs = jnp.einsum("ij,jp->ip", scores, weighted, precision=precise)
    outputs = outputs + jnp.exp(log_keep)[:, None] * jnp.einsum(
        "in,pn->ip", c_rows, state_in, precision=precise
    )
    remains = jnp.exp(log_keep[-1] - log_keep)
    state_out = jnp.exp(log_keep[-1]) * state_in + jnp.einsum(
        "j,jp,jn->pn", remains, weighted, b_rows, precision=precise
    )
    return (outputs, state_out)


def strand_core(x_ext, gate_in, b_c, dt_raw, state_in, params):
    dt_bias_h, decay_rate, skip_h, conv_w = params
    conv_out = conv_silu(x_ext, conv_w)
    steps_dt = jax.nn.softplus(dt_raw + dt_bias_h)
    outputs, state_out = block_ssd(
        conv_out, steps_dt, b_c[:, :STATE], b_c[:, STATE:], decay_rate, state_in
    )
    gated = (outputs + skip_h * conv_out) * jax.nn.silu(gate_in)
    return (gated, state_out)


def strand_summary(x_ext, b_c, dt_raw, params):
    dt_bias_h, decay_rate, skip_h, conv_w = params
    conv_out = conv_silu(x_ext, conv_w)
    steps_dt = jax.nn.softplus(dt_raw + dt_bias_h)
    log_keep = jnp.cumsum(steps_dt * decay_rate)
    remains = jnp.exp(log_keep[-1] - log_keep) * steps_dt
    local_state = jnp.einsum("j,jp,jn->pn", remains, conv_out, b_c[:, :STATE], precision=precise)
    return (jnp.exp(log_keep[-1]), local_state)


def chain_step(earlier, following):
    return (earlier[0] * following[0], following[0] * earlier[1] + following[1])


def local(hidden, w_in, w_bc, w_dt, dt_bias, a_log, d_skip, conv_w, w_out, d_out):
    own_rows = hidden.shape[0]
    seq_rows = own_rows * lax.axis_size("tp")
    length_all = seq_rows * lax.axis_size("ctx")
    head_dim = w_out.shape[0]
    rim_rows = CONV - 1
    w_pair = jnp.concatenate([w_in, w_in[::-1]], axis=1)
    bc_pair = jnp.concatenate([w_bc, w_bc[::-1]], axis=1)
    dt_pair = jnp.concatenate([w_dt, w_dt[:, ::-1]], axis=0)
    out_pair = jnp.concatenate([w_out, w_out[:, ::-1]], axis=0)
    params = (dt_bias[0], -jnp.exp(a_log[0]), d_skip[0], conv_w)
    gathered = lax.all_gather(hidden, "tp", axis=0, tiled=True)
    projected = jnp.dot(gathered, w_pair, preferred_element_type=jnp.float32).astype(jnp.bfloat16)
    dt_raw = times_rows(gathered, dt_pair)
    b_c_all = jnp.dot(gathered, bc_pair, preferred_element_type=jnp.float32)
    x_both = jnp.concatenate(
        [projected[:, :head_dim], projected[:, 2 * head_dim : 3 * head_dim]], axis=1
    )
    x_halo = padded(x_both, (("ctx", 0),), rim_rows).astype(jnp.float32)
    x_ext = jnp.stack(
        [x_halo[: seq_rows + rim_rows, :head_dim], x_halo[rim_rows:, head_dim:][::-1]]
    )
    gate_in = jnp.stack(
        [projected[:, head_dim : 2 * head_dim], projected[::-1, 3 * head_dim :]]
    ).astype(jnp.float32)
    b_c = jnp.stack([b_c_all[:, : 2 * STATE], b_c_all[::-1, 2 * STATE :]])
    dt_both = jnp.stack([dt_raw[:, 0], dt_raw[::-1, 1]])
    decays, local_states = jax.vmap(strand_summary, in_axes=(0, 0, 0, None))(
        x_ext, b_c, dt_both, params
    )
    identity = (jnp.ones((), jnp.float32), jnp.zeros((head_dim, STATE), jnp.float32))
    fwd_in = entering((decays[0], local_states[0]), "ctx", chain_step, identity, False)[1]
    rev_in = entering((decays[1], local_states[1]), "ctx", chain_step, identity, True)[1]
    states_in = jnp.stack([fwd_in, rev_in])

    def core_both(x_part, gate_part, bc_part, dt_part, state_part):
        return jax.vmap(strand_core, in_axes=(0, 0, 0, 0, 0, None))(
            x_part, gate_part, bc_part, dt_part, state_part, params
        )

    (gated, states_out), pullback = jax.vjp(core_both, x_ext, gate_in, b_c, dt_both, states_in)
    gated_nat = jnp.concatenate([gated[0], gated[1][::-1]], axis=1).astype(jnp.bfloat16)
    portion = lax.all_gather(d_out, "tp", axis=0, tiled=True)
    grads_g = times_rows(portion, out_pair)
    grad_wout = across_rows(gated_nat, portion)
    grad_stack = jnp.stack([grads_g[:, :head_dim], grads_g[::-1, head_dim:]])
    direct = pullback((grad_stack, jnp.zeros_like(states_out)))
    direct_state = direct[4]
    fwd_adj = entering((decays[0], direct_state[0]), "ctx", chain_step, identity, True)[1]
    rev_adj = entering((decays[1], direct_state[1]), "ctx", chain_step, identity, False)[1]
    carried_grads = pullback((jnp.zeros_like(gated), jnp.stack([fwd_adj, rev_adj])))
    grad_x = direct[0] + carried_grads[0]
    grad_gates = direct[1] + carried_grads[1]
    grad_bcs = direct[2] + carried_grads[2]
    grad_dts = direct[3] + carried_grads[3]
    grad_x_rev = grad_x[1][::-1]
    grad_x_local = jnp.concatenate([grad_x[0][rim_rows:], grad_x_rev[:seq_rows]], axis=1)
    outgoing = jnp.concatenate([grad_x[0][:rim_rows], grad_x_rev[seq_rows:]], axis=0)
    incoming = padded(outgoing, (("ctx", 0),), rim_rows)
    grad_x_local = grad_x_local.at[:rim_rows, head_dim:].add(incoming[:rim_rows])
    grad_x_local = grad_x_local.at[seq_rows - rim_rows :, :head_dim].add(incoming[3 * rim_rows :])
    grad_proj = jnp.concatenate(
        [
            grad_x_local[:, :head_dim],
            grad_gates[0],
            grad_x_local[:, head_dim:],
            grad_gates[1][::-1],
        ],
        axis=1,
    ).astype(jnp.bfloat16)
    grad_bc = jnp.concatenate([grad_bcs[0], grad_bcs[1][::-1]], axis=1).astype(jnp.bfloat16)
    grad_dt = jnp.stack([grad_dts[0], grad_dts[1][::-1]], axis=1).astype(jnp.bfloat16)

    def strand_term(which):
        proj_cols = grad_proj[:, which * 2 * head_dim : (which + 1) * 2 * head_dim]
        wide_cols = w_pair[:, which * 2 * head_dim : (which + 1) * 2 * head_dim]
        bc_cols = grad_bc[:, which * 2 * STATE : (which + 1) * 2 * STATE]
        shared_cols = bc_pair[:, which * 2 * STATE : (which + 1) * 2 * STATE]
        dt_cols = grad_dt[:, which : which + 1]
        dt_rows = dt_pair[which : which + 1]
        summed = times_rows(proj_cols, wide_cols) + times_rows(bc_cols, shared_cols)
        return summed + jnp.dot(dt_cols, dt_rows, preferred_element_type=jnp.float32)

    forward_part = lax.psum_scatter(strand_term(0), "tp", scatter_dimension=0, tiled=True)
    reverse_part = lax.psum_scatter(strand_term(1), "tp", scatter_dimension=0, tiled=True)
    d_hidden = (forward_part + reverse_part).astype(jnp.bfloat16)
    scaling = 1.0 / math.sqrt(length_all)
    grad_pair = across_rows(gathered, grad_proj)
    d_w_in = (grad_pair[:, : 2 * head_dim] + grad_pair[::-1, 2 * head_dim :]) * scaling
    d_w_out = (grad_wout[:head_dim] + grad_wout[head_dim:, ::-1]) * scaling
    d_w_in, d_w_out = (
        lax.psum(d_w_in.astype(jnp.bfloat16), "ctx").astype(jnp.float32),
        lax.psum(d_w_out.astype(jnp.bfloat16), "ctx").astype(jnp.float32),
    )
    grad_bpair = across_rows(gathered, grad_bc)
    d_w_bc = lax.psum(
        (grad_bpair[:, : 2 * STATE] + grad_bpair[::-1, 2 * STATE :]) * scaling, ("ctx", "tp")
    )
    return (d_hidden, d_w_in, d_w_out, d_w_bc)


def solution(mesh):
    in_specs = (
        P(("ctx", "tp"), None),
        P(None, "tp"),
        P(),
        P("tp", None),
        P("tp"),
        P("tp"),
        P("tp"),
        P(None, "tp"),
        P("tp", None),
        P(("ctx", "tp"), None),
    )
    out_specs = (P(("ctx", "tp"), None), P(None, "tp"), P("tp", None), P())
    return jax.shard_map(local, mesh=mesh, in_specs=in_specs, out_specs=out_specs, check_vma=False)
```

profile of v0, /device:TPU:4, one launch (start us, length us, event | category | flops | bytes accessed | tf_op | source)
XLA Modules:
  0.0 1343.6 jit_solution(9077498691237861709)
XLA Ops:
  8.7 6.0 rev.53
  14.8 1.3 convert.70
  18.7 1.3 and_reduce_fusion
  20.6 1.4 slice_bitcast_fusion.12
  22.6 6.3 rev.55
  29.0 8.4 rev.49
  37.4 6.3 rev.51
  43.7 1.3 dynamic-slice.21
  45.7 1.3 dynamic-slice.19
  47.0 85.0 %all-gather.7.cloned.1.call-done = bf16[64,4,2048]{2,1,0:T(4,128)(2,1)} async-done(((bf16[1,4,2048]{2,1,0:T(4,128)(2,1)}), bf16[64,4,2048]{2,1,0:T(4,128)(2,1)}) %all-gather.7.cloned.1.call-update) | async-done | bytes 1048592 | tf_op jit(solution)/shard_map/all_gather | solution.py:119
  132.1 1.3 reshape.271
  138.8 2.1 slice_dynamic-update-slice_fusion
  141.6 107.5 %all-gather.5.cloned.1.call-done = bf16[64,4,2048]{2,1,0:T(4,128)(2,1)} async-done(((bf16[1,4,2048]{2,1,0:T(4,128)(2,1)}), bf16[64,4,2048]{2,1,0:T(4,128)(2,1)}) %all-gather.5.cloned.1.call-update) | async-done | bytes 1048592 | tf_op jit(solution)/shard_map/all_gather | solution.py:150
  249.2 1.3 reshape.269
  250.5 1.5 convolution_bitcast_fusion.2
  253.1 8.6 collective-permute-start
  261.7 1.3 collective-permute-start.1
  263.8 0.9 convolution_add_fusion.9
  264.7 68.7 %all_gather.29 = f32[8,64,16]{1,2,0:T(8,128)S(1)} all-gather(f32[1,64,16]{1,2,0:T(8,128)S(1)} %get-tuple-element.678), channel_id=1, replica_groups=mesh['ctx'=8,'tp'=64] {'ctx'}, dimensions={0}, use_global_device_ids=true | all-gather | bytes 36864 | tf_op jit(solution)/shard_map/all_gather | solution.py:27
  333.4 41.5 %all-reduce.19 = (f32[8]{0:T(128)S(1)}, f32[8]{0:T(128)S(1)}) all-reduce(f32[8]{0:T(128)} %slice_dynamic-update-slice_fusion, f32[8]{0:T(128)} %copy-done.65), channel_id=1, replica_groups=mesh['ctx'=8,'tp'=64] {'ctx'}, use_global_device_ids=true, to_apply=%add.17 | all-reduce | flops 16 | bytes 128
  374.9 10.2 while.62
  385.1 63.2 %all_gather.31 = f32[8,64,16]{1,2,0:T(8,128)S(1)} all-gather(f32[1,64,16]{1,2,0:T(8,128)S(1)} %get-tuple-element.679), channel_id=1, replica_groups=mesh['ctx'=8,'tp'=64] {'ctx'}, dimensions={0}, use_global_device_ids=true | all-gather | bytes 36864 | tf_op jit(solution)/shard_map/all_gather | solution.py:27
  448.3 10.1 while.63
  459.6 0.9 multiply_reduce_fusion.5
  461.9 63.1 %all_gather.32 = f32[8,64,16]{1,2,0:T(8,128)S(1)} all-gather(f32[1,64,16]{1,2,0:T(8,128)S(1)} %get-tuple-element.676), channel_id=1, replica_groups=mesh['ctx'=8,'tp'=64] {'ctx'}, dimensions={0}, use_global_device_ids=true | all-gather | bytes 36864 | tf_op jit(solution)/shard_map/all_gather | solution.py:27
  525.1 10.1 while.64
  535.2 63.3 %all_gather.33 = f32[8,64,16]{1,2,0:T(8,128)S(1)} all-gather(f32[1,64,16]{1,2,0:T(8,128)S(1)} %get-tuple-element.677), channel_id=1, replica_groups=mesh['ctx'=8,'tp'=64] {'ctx'}, dimensions={0}, use_global_device_ids=true | all-gather | bytes 36864 | tf_op jit(solution)/shard_map/all_gather | solution.py:27
  598.4 10.2 while.65
  609.9 1.3 fusion.101
  611.2 1.3 fusion.92
  612.6 1.3 fusion.23
  613.9 1.2 convolution_add_fusion.7
  615.1 1.6 fusion.127
  616.6 1.3 fusion.26
  618.7 1.4 multiply_reduce_fusion.3
  621.3 1.3 copy.40
  622.6 1.3 copy.38
  625.4 1.4 convolution_add_fusion.8
  626.9 1.0 convolution_add_fusion.6
  627.8 2.1 fusion.188
  631.5 2.5 reduce-window.24
  634.9 2.5 reduce-window.26
  639.1 1.1 fusion.112
  640.2 1.3 rev.63
  642.6 0.8 slice.317
  643.4 2.5 collective-permute-start.2
  645.9 1.5 collective-permute-start.3
  648.1 1.1 convolution_bitcast_fusion.1
  649.3 1.9 add_select_fusion
  651.2 2.0 scatter-add.6
  653.2 7.6 collective-permute-done.3
  660.8 1.1 scatter-add.9
  662.0 1.2 convolution_bitcast_fusion
  663.2 1.0 slice.386
  664.2 7.5 rev.61
  671.7 0.9 fusion.10
  672.7 0.8 fusion.157
  673.7 1.2 rev.64
  674.8 1.7 fusion.31
  678.8 453.5 %all-reduce.28 = bf16[256,2048]{1,0:T(8,128)(2,1)S(1)} all-reduce(f32[256,2048]{1,0:T(8,128)S(1)} %fusion.6), channel_id=3, replica_groups=mesh['ctx'=8,'tp'=64] {'tp'}, use_global_device_ids=true, to_apply=%region_27.28.clone | all-reduce | flops 524288 | bytes 3145728
  1133.0 2.2 copy.41
  1135.2 1.8 convert_element_type.39
  1137.0 198.5 %all-reduce.25.cloned.1.call-done = f32[2048,32]{0,1:T(8,128)} async-done(((f32[2048,32]{0,1:T(8,128)}), f32[2048,32]{0,1:T(8,128)}) %all-reduce.25.cloned.1.call-update) | async-done | bytes 262160 | tf_op jit(solution)/shard_map/psum | solution.py:203
  1335.4 1.7 copy.111
  (305 shorter events, 66.8 us)
Async XLA Ops:
  7.2 126.2 %copy-start.27 = (bf16[1,2048]{1,0:T(2,128)(2,1)S(1)}, bf16[1,2048]{1,0:T(2,128)(2,1)}, u32[]{:S(2)}) copy-start(bf16[1,2048]{1,0:T(2,128)(2,1)} %param.25) | copy-start | bytes 12292
  7.2 124.9 %all-gather.7.cloned.1.call-start = ((), (), s32[]{:S(2)}) async-start(), calls=%async_computation.2 | async-start | bytes 1064960 | tf_op jit(solution)/shard_map/all_gather | solution.py:119
  7.9 241.2 %all-gather.5.cloned.1.call-start = ((), (), s32[]{:S(2)}) async-start(), calls=%async_computation.1 | async-start | bytes 1064960 | tf_op jit(solution)/shard_map/all_gather | solution.py:150
  8.7 1124.3 %all-reduce.27.cloned.1.call-start = ((), (), s32[]{:S(2)}) async-start(), calls=%async_computation.3 | async-start | bytes 1572864 | tf_op jit(solution)/shard_map/psum | solution.py:199
  29.0 106.7 %copy-start.5 = (bf16[2048,32]{0,1:T(8,128)(2,1)}, bf16[2048,32]{0,1:T(8,128)(2,1)S(1)}, u32[]{:S(2)}) copy-start(bf16[2048,32]{0,1:T(8,128)(2,1)S(1)} %rev.55) | copy-start | bytes 393220
  37.4 98.3 %copy-start.4 = (bf16[2048,32]{0,1:T(8,128)(2,1)S(1)}, bf16[2048,32]{0,1:T(8,128)(2,1)}, u32[]{:S(2)}) copy-start(bf16[2048,32]{0,1:T(8,128)(2,1)} %param.24) | copy-start | bytes 393220
  43.7 208.6 %copy-start.2 = (bf16[2048,128]{1,0:T(8,128)(2,1)}, bf16[2048,128]{1,0:T(8,128)(2,1)S(1)}, u32[]{:S(2)}) copy-start(bf16[2048,128]{1,0:T(8,128)(2,1)S(1)} %rev.51) | copy-start | bytes 1572868
  134.6 326.7 %copy-start.33 = (f32[256,1]{0,1:T(1,128)}, f32[256,1]{0,1:T(1,128)S(1)}, u32[]{:S(2)}) copy-start(f32[256,1]{0,1:T(1,128)S(1)} %rev.54) | copy-start | bytes 3076
  135.6 116.4 %copy-start.48 = (f32[1,2,2,128]{3,1,2,0:T(2,128)}, f32[1,2,2,128]{3,1,2,0:T(2,128)S(1)}, u32[]{:S(2)}) copy-start(f32[1,2,2,128]{3,1,2,0:T(2,128)S(1)} %copy.67) | copy-start | bytes 6148
  137.7 114.4 %copy-start.63 = (f32[2]{0:T(128)}, f32[2]{0:T(128)S(1)}, u32[]{:S(2)}) copy-start(f32[2]{0:T(128)S(1)} %slice_reduce_fusion.3) | copy-start | bytes 28
  141.6 110.5 %copy-start.65 = (f32[8]{0:T(128)}, f32[8]{0:T(128)S(1)}, u32[]{:S(2)}) copy-start(f32[8]{0:T(128)S(1)} %slice_dynamic-update-slice_fusion.1) | copy-start | bytes 100
  141.6 110.6 %copy-start = (bf16[2048,128]{1,0:T(8,128)(2,1)S(1)}, bf16[2048,128]{1,0:T(8,128)(2,1)}, u32[]{:S(2)}) copy-start(bf16[2048,128]{1,0:T(8,128)(2,1)} %param.23) | copy-start | bytes 1572868
  252.1 11.7 copy-start.15
  252.3 12.4 copy-start.14
  252.3 206.2 %copy-start.34 = (f32[1,256]{1,0:T(1,128)S(1)}, f32[1,256]{1,0:T(1,128)}, u32[]{:S(2)}) copy-start(f32[1,256]{1,0:T(1,128)} %get-tuple-element.686) | copy-start | bytes 3076
  252.8 206.3 %copy-start.42 = (f32[64]{0:T(128)S(1)}, f32[64]{0:T(128)}, u32[]{:S(2)}) copy-start(f32[64]{0:T(128)} %get-tuple-element.689) | copy-start | bytes 772
  252.8 206.3 %copy-start.44 = (f32[64]{0:T(128)S(1)}, f32[64]{0:T(128)}, u32[]{:S(2)}) copy-start(f32[64]{0:T(128)} %get-tuple-element.690) | copy-start | bytes 772
  252.8 206.3 %copy-start.46 = (f32[64]{0:T(128)S(1)}, f32[64]{0:T(128)}, u32[]{:S(2)}) copy-start(f32[64]{0:T(128)} %get-tuple-element.691) | copy-start | bytes 772
  252.8 206.3 %copy-start.53 = (f32[64]{0:T(128)S(1)}, f32[64]{0:T(128)}, u32[]{:S(2)}) copy-start(f32[64]{0:T(128)} %get-tuple-element.688) | copy-start | bytes 772
  252.8 206.8 %copy-start.21 = (f32[256,32]{0,1:T(8,128)S(1)}, f32[256,32]{0,1:T(8,128)}, u32[]{:S(2)}) copy-start(f32[256,32]{0,1:T(8,128)} %rev.56) | copy-start | bytes 98308
  252.8 206.8 %copy-start.23 = (f32[1,256,32]{1,2,0:T(8,128)S(1)}, f32[1,256,32]{1,2,0:T(8,128)}, u32[]{:S(2)}) copy-start(f32[1,256,32]{1,2,0:T(8,128)} %get-tuple-element.672) | copy-start | bytes 98308
  252.9 205.7 %copy-start.24 = (bf16[1,256,64]{1,2,0:T(8,128)(2,1)}, bf16[1,256,64]{1,2,0:T(8,128)(2,1)S(1)}, u32[]{:S(2)}) copy-start(bf16[1,256,64]{1,2,0:T(8,128)(2,1)S(1)} %get-tuple-element.658) | copy-start | bytes 98308
  253.1 205.5 %copy-start.18 = (bf16[256,64]{0,1:T(8,128)(2,1)}, bf16[256,64]{0,1:T(8,128)(2,1)S(1)}, u32[]{:S(2)}) copy-start(bf16[256,64]{0,1:T(8,128)(2,1)S(1)} %rev.52) | copy-start | bytes 98308
  253.1 205.4 %collective-permute-start = (bf16[3,128]{0,1:T(8,128)(2,1)S(1)}, bf16[3,128]{0,1:T(8,128)(2,1)S(1)}, u32[]{:S(2)}, u32[]{:S(2)}) collective-permute-start(bf16[3,128]{0,1:T(8,128)(2,1)S(1)} %get-tuple-element.670), channel_id=1, source_target_pairs={{0,64},{64,128},{128,192},{192,256},{256,320},{320,384},{384,448},... | collective-permute-start | bytes 2312 | tf_op jit(solution)/shard_map/ppermute | solution.py:19
  261.7 196.8 %collective-permute-start.1 = (bf16[3,128]{0,1:T(8,128)(2,1)S(1)}, bf16[3,128]{0,1:T(8,128)(2,1)S(1)}, u32[]{:S(2)}, u32[]{:S(2)}) collective-permute-start(bf16[3,128]{0,1:T(8,128)(2,1)S(1)} %get-tuple-element.671), channel_id=1, source_target_pairs={{64,0},{128,64},{192,128},{256,192},{320,256},{384,320},{448,384},... | collective-permute-start | bytes 2312 | tf_op jit(solution)/shard_map/ppermute | solution.py:20
  263.7 196.8 %copy-start.64 = (f32[2]{0:T(128)S(1)}, f32[2]{0:T(128)}, u32[]{:S(2)}) copy-start(f32[2]{0:T(128)} %copy-done.63) | copy-start | bytes 28
  263.7 197.5 %copy-start.35 = (f32[1,256]{1,0:T(1,128)S(1)}, f32[1,256]{1,0:T(1,128)}, u32[]{:S(2)}) copy-start(f32[1,256]{1,0:T(1,128)} %get-tuple-element.686) | copy-start | bytes 3076
  458.5 140.0 %copy-start.36 = (f32[2,256]{1,0:T(2,128)}, f32[2,256]{1,0:T(2,128)S(1)}, u32[]{:S(2)}) copy-start(f32[2,256]{1,0:T(2,128)S(1)} %compare_select_fusion.3) | copy-start | bytes 6148
  459.3 151.9 %copy-start.19 = (bf16[256,64]{0,1:T(8,128)(2,1)S(1)}, bf16[256,64]{0,1:T(8,128)(2,1)}, u32[]{:S(2)}) copy-start(bf16[256,64]{0,1:T(8,128)(2,1)} %copy-done.18) | copy-start | bytes 98308
  459.4 151.9 %copy-start.25 = (bf16[1,256,64]{1,2,0:T(8,128)(2,1)S(1)}, bf16[1,256,64]{1,2,0:T(8,128)(2,1)}, u32[]{:S(2)}) copy-start(bf16[1,256,64]{1,2,0:T(8,128)(2,1)} %copy-done.24) | copy-start | bytes 98308
  460.5 152.1 %copy-start.28 = (pred[256,256]{1,0:T(8,128)(4,1)S(1)}, pred[256,256]{1,0:T(8,128)(4,1)}, u32[]{:S(2)}) copy-start(pred[256,256]{1,0:T(8,128)(4,1)} %iota_compare_fusion) | copy-start | bytes 196612
  460.5 152.1 %copy-start.49 = (f32[1,2,2,128]{3,1,2,0:T(2,128)S(1)}, f32[1,2,2,128]{3,1,2,0:T(2,128)}, u32[]{:S(2)}) copy-start(f32[1,2,2,128]{3,1,2,0:T(2,128)} %copy-done.48) | copy-start | bytes 6148
  609.6 9.0 copy-start.22
  615.1 3.6 copy-start.29
  615.1 3.6 copy-start.37
  615.1 3.6 copy-start.50
  615.1 3.6 copy-start.54
  625.3 4.7 copy-start.39
  625.3 4.7 copy-start.41
  625.4 4.7 copy-start.55
  625.4 4.7 copy-start.56
  625.4 4.7 copy-start.57
  625.4 4.7 copy-start.58
  625.4 4.7 copy-start.59
  625.4 4.7 copy-start.60
  625.4 4.7 copy-start.61
  625.4 4.7 copy-start.62
  626.8 4.2 copy-start.20
  626.8 4.2 copy-start.26
  626.8 4.2 copy-start.67
  627.8 3.4 copy-start.32
  631.0 31.0 %copy-start.7 = (bf16[256,64]{0,1:T(8,128)(2,1)}, bf16[256,64]{0,1:T(8,128)(2,1)S(1)}, u32[]{:S(2)}) copy-start(bf16[256,64]{0,1:T(8,128)(2,1)S(1)} %rev.58) | copy-start | bytes 98308
  631.3 16.8 %copy-start.16 = (bf16[256,32]{0,1:T(8,128)(2,1)}, bf16[256,32]{0,1:T(8,128)(2,1)S(1)}, u32[]{:S(2)}) copy-start(bf16[256,32]{0,1:T(8,128)(2,1)S(1)} %get-tuple-element.674) | copy-start | bytes 49156
  640.2 7.2 copy-start.51
  640.2 7.2 copy-start.52
  643.4 5.8 collective-permute-start.2
  645.9 14.8 %collective-permute-start.3 = (f32[3,64]{0,1:T(8,128)}, f32[3,64]{0,1:T(8,128)S(1)}, u32[]{:S(2)}, u32[]{:S(2)}) collective-permute-start(f32[3,64]{0,1:T(8,128)} %get-tuple-element.638), channel_id=1, source_target_pairs={{64,0},{128,64},{192,128},{256,192},{320,256},{384,320},{448,384},... | collective-permute-start | bytes 2312 | tf_op jit(solution)/shard_map/ppermute | solution.py:20
  672.7 3.9 copy-start.3
  672.7 3.9 copy-start.8
  672.7 3.9 copy-start.12
  672.7 662.7 %all-reduce.25.cloned.1.call-start = ((), (), s32[]{:S(2)}) async-start(), calls=%async_computation | async-start | bytes 524288 | tf_op jit(solution)/shard_map/psum | solution.py:203
  673.6 3.4 copy-start.1
  673.6 3.5 copy-start.10
  673.6 3.5 copy-start.13
  (13 other events, 21.7 us)
Sparse Core Ops, SparseCore 0:
  10.2 121.8 all-gather.6
  134.2 114.9 all-gather.4
  672.8 200.6 all-reduce.26
  879.7 455.7 all-reduce.24
where the time goes:
time: 1350 us; the launch traced here: 1340 us
  blocking collectives  753 us (56%)
  waiting for transfers between devices  400 us (30%)
  local copies, waits for them, and re-layouts  87.5 us (6%)
  other arithmetic  44.4 us (3%)
  matrix products  25.8 us (2%)
  between operations  17.6 us (1%)
  starting transfers between devices  14 us (1%)
    unnamed x2, blocking collectives  495 us
    all_gather x4, blocking collectives, entering(): everything = jax.tree.map(lambda part: lax.all_gather(part, axis), array)  258 us
    psum x1, waiting for transfers between devices, local(): lax.psum((grad_bpair[:, :2 * STATE] + grad_bpair[::-1, 2 * STATE:]) * sca...  198 us
    all_gather x1, waiting for transfers between devices, local(): portion = lax.all_gather(d_out, 'tp', axis=0, tiled=True)  108 us
    all_gather x1, waiting for transfers between devices, local(): gathered = lax.all_gather(hidden, 'tp', axis=0, tiled=True)  85 us
  transfers between devices with their start and end apart: 8, of which 4 were waited for; matrix products, arithmetic and copies ran while one was open for 6% of the time, Pallas kernels for 0%

commit v1 on v0

--- a/solution.py
+++ b/solution.py
@@ -201,7 +201,8 @@
     )
     grad_bpair = across_rows(gathered, grad_bc)
     d_w_bc = lax.psum(
-        (grad_bpair[:, : 2 * STATE] + grad_bpair[::-1, 2 * STATE :]) * scaling, ("ctx", "tp")
+        lax.psum((grad_bpair[:, : 2 * STATE] + grad_bpair[::-1, 2 * STATE :]) * scaling, "tp"),
+        "ctx",
     )
     return (d_hidden, d_w_in, d_w_out, d_w_bc)
 

time: 1350 us -> 1950 us (1.44)
  the two profiles are of different devices: /device:TPU:4 before, /device:TPU:256 now
where the time goes in v1:
time: 1950 us; the launch traced here: 1940 us
  waiting for transfers between devices  934 us (48%)
  blocking collectives  792 us (41%)
  local copies, waits for them, and re-layouts  88.4 us (5%)
  other arithmetic  48.6 us (2%)
  matrix products  30.6 us (2%)
  starting transfers between devices  29.5 us (2%)
    psum x1, waiting for transfers between devices, local(): lax.psum((grad_bpair[:, :2 * STATE] + grad_bpair[::-1, 2 * STATE:]) * sca...  737 us
    unnamed x2, blocking collectives  542 us
    all_gather x4, blocking collectives, entering(): everything = jax.tree.map(lambda part: lax.all_gather(part, axis), array)  251 us
    all_gather x1, waiting for transfers between devices, local(): portion = lax.all_gather(d_out, 'tp', axis=0, tiled=True)  108 us
    all_gather x1, waiting for transfers between devices, local(): gathered = lax.all_gather(hidden, 'tp', axis=0, tiled=True)  79.6 us
  transfers between devices with their start and end apart: 9, of which 4 were waited for; matrix products, arithmetic and copies ran while one was open for 5% of the time, Pallas kernels for 0%

profile of v1, /device:TPU:256, one launch (start us, length us, event | category | flops | bytes accessed | tf_op | source)
XLA Modules:
  0.0 1941.8 jit_solution(7818732956382641588)
XLA Ops:
  8.7 6.0 rev.53
  14.8 1.3 convert.70
  18.7 1.3 and_reduce_fusion
  20.7 1.4 slice_bitcast_fusion.12
  22.7 6.3 rev.55
  29.1 8.4 rev.49
  37.5 6.3 rev.51
  43.8 1.3 dynamic-slice.21
  45.8 1.3 dynamic-slice.19
  47.1 79.6 %all-gather.7.cloned.1.call-done = bf16[64,4,2048]{2,1,0:T(4,128)(2,1)} async-done(((bf16[1,4,2048]{2,1,0:T(4,128)(2,1)}), bf16[64,4,2048]{2,1,0:T(4,128)(2,1)}) %all-gather.7.cloned.1.call-update) | async-done | bytes 1048592 | tf_op jit(solution)/shard_map/all_gather | solution.py:119
  126.7 1.3 reshape.271
  132.8 2.0 slice_dynamic-update-slice_fusion
  135.6 108.3 %all-gather.5.cloned.1.call-done = bf16[64,4,2048]{2,1,0:T(4,128)(2,1)} async-done(((bf16[1,4,2048]{2,1,0:T(4,128)(2,1)}), bf16[64,4,2048]{2,1,0:T(4,128)(2,1)}) %all-gather.5.cloned.1.call-update) | async-done | bytes 1048592 | tf_op jit(solution)/shard_map/all_gather | solution.py:150
  243.8 1.3 reshape.269
  245.2 1.5 convolution_bitcast_fusion.2
  247.4 0.9 rev.50
  249.1 7.0 collective-permute-start
  256.2 7.5 collective-permute-start.1
  264.4 0.9 fusion.95
  266.2 63.1 %all_gather.29 = f32[8,64,16]{1,2,0:T(8,128)S(1)} all-gather(f32[1,64,16]{1,2,0:T(8,128)S(1)} %get-tuple-element.678), channel_id=1, replica_groups=mesh['ctx'=8,'tp'=64] {'ctx'}, dimensions={0}, use_global_device_ids=true | all-gather | bytes 36864 | tf_op jit(solution)/shard_map/all_gather | solution.py:27
  329.3 38.8 %all-reduce.19 = (f32[8]{0:T(128)S(1)}, f32[8]{0:T(128)S(1)}) all-reduce(f32[8]{0:T(128)} %slice_dynamic-update-slice_fusion, f32[8]{0:T(128)} %copy-done.51), channel_id=1, replica_groups=mesh['ctx'=8,'tp'=64] {'ctx'}, use_global_device_ids=true, to_apply=%add.17 | all-reduce | flops 16 | bytes 128
  368.1 10.2 while.62
  378.3 61.0 %all_gather.31 = f32[8,64,16]{1,2,0:T(8,128)S(1)} all-gather(f32[1,64,16]{1,2,0:T(8,128)S(1)} %get-tuple-element.679), channel_id=1, replica_groups=mesh['ctx'=8,'tp'=64] {'ctx'}, dimensions={0}, use_global_device_ids=true | all-gather | bytes 36864 | tf_op jit(solution)/shard_map/all_gather | solution.py:27
  439.3 10.1 while.63
  450.1 0.9 fusion.74
  451.2 1.6 multiply_reduce_fusion.5
  454.3 63.1 %all_gather.32 = f32[8,64,16]{1,2,0:T(8,128)S(1)} all-gather(f32[1,64,16]{1,2,0:T(8,128)S(1)} %get-tuple-element.676), channel_id=1, replica_groups=mesh['ctx'=8,'tp'=64] {'ctx'}, dimensions={0}, use_global_device_ids=true | all-gather | bytes 36864 | tf_op jit(solution)/shard_map/all_gather | solution.py:27
  517.3 10.1 while.64
  527.5 63.2 %all_gather.33 = f32[8,64,16]{1,2,0:T(8,128)S(1)} all-gather(f32[1,64,16]{1,2,0:T(8,128)S(1)} %get-tuple-element.677), channel_id=1, replica_groups=mesh['ctx'=8,'tp'=64] {'ctx'}, dimensions={0}, use_global_device_ids=true | all-gather | bytes 36864 | tf_op jit(solution)/shard_map/all_gather | solution.py:27
  590.7 10.2 while.65
  601.0 1.0 fusion.153
  602.0 0.9 fusion.142
  602.9 1.3 fusion.101
  604.2 1.3 fusion.92
  605.5 2.2 fusion.23
  607.7 2.0 convolution_add_fusion.7
  609.8 2.2 fusion.127
  612.0 1.3 fusion.26
  615.0 1.7 convolution_add_fusion.3
  616.7 3.2 multiply_reduce_fusion.3
  621.3 2.5 reduce-window.24
  625.5 2.5 reduce-window.26
  632.2 1.2 broadcast_multiply_fusion
  634.1 1.1 add_add_fusion
  635.2 1.3 convolution_add_fusion.8
  640.2 1.2 rev.64
  642.2 1.1 fusion.112
  643.4 1.3 rev.63
  645.4 1.0 slice_bitcast_fusion.4
  647.5 10.4 collective-permute-start.2
  657.9 4.3 collective-permute-start.3
  662.3 2.1 add_select_fusion
  664.4 2.1 scatter-add.6
  666.5 7.3 collective-permute-done.3
  673.9 1.1 scatter-add.9
  675.5 1.0 slice.386
  676.5 7.5 rev.61
  684.0 0.9 fusion.10
  684.9 1.6 fusion.108
  688.4 737.5 %all-reduce.26.cloned.1.call-done = f32[2048,32]{0,1:T(8,128)} async-done(((f32[2048,32]{0,1:T(8,128)}), f32[2048,32]{0,1:T(8,128)}) %all-reduce.26.cloned.1.call-update) | async-done | bytes 262160 | tf_op jit(solution)/shard_map/psum | solution.py:204
  1425.9 503.0 %all-reduce.31 = bf16[256,2048]{1,0:T(8,128)(2,1)S(1)} all-reduce(f32[256,2048]{1,0:T(8,128)S(1)} %fusion.6), channel_id=3, replica_groups=mesh['ctx'=8,'tp'=64] {'tp'}, use_global_device_ids=true, to_apply=%region_27.28.clone | all-reduce | flops 524288 | bytes 3145728
  1929.6 2.2 copy.41
  1931.8 1.8 convert_element_type.39
  1933.6 1.7 copy.112
  (283 shorter events, 72.7 us)
Async XLA Ops:
  7.2 120.9 %copy-start.18 = (bf16[1,2048]{1,0:T(2,128)(2,1)S(1)}, bf16[1,2048]{1,0:T(2,128)(2,1)}, u32[]{:S(2)}) copy-start(bf16[1,2048]{1,0:T(2,128)(2,1)} %param.25) | copy-start | bytes 12292
  7.2 119.5 %all-gather.7.cloned.1.call-start = ((), (), s32[]{:S(2)}) async-start(), calls=%async_computation.3 | async-start | bytes 1064960 | tf_op jit(solution)/shard_map/all_gather | solution.py:119
  7.9 235.9 %all-gather.5.cloned.1.call-start = ((), (), s32[]{:S(2)}) async-start(), calls=%async_computation.2 | async-start | bytes 1064960 | tf_op jit(solution)/shard_map/all_gather | solution.py:150
  8.7 1417.3 %all-reduce.26.cloned.1.call-start = ((), (), s32[]{:S(2)}) async-start(), calls=%async_computation | async-start | bytes 524288 | tf_op jit(solution)/shard_map/psum | solution.py:204
  37.5 92.2 %copy-start.3 = (bf16[2048,32]{0,1:T(8,128)(2,1)S(1)}, bf16[2048,32]{0,1:T(8,128)(2,1)}, u32[]{:S(2)}) copy-start(bf16[2048,32]{0,1:T(8,128)(2,1)} %param.24) | copy-start | bytes 393220
  43.8 205.0 %copy-start.2 = (bf16[2048,128]{1,0:T(8,128)(2,1)}, bf16[2048,128]{1,0:T(8,128)(2,1)S(1)}, u32[]{:S(2)}) copy-start(bf16[2048,128]{1,0:T(8,128)(2,1)S(1)} %rev.51) | copy-start | bytes 1572868
  128.4 321.0 %copy-start.25 = (f32[1,256]{1,0:T(1,128)}, f32[1,256]{1,0:T(1,128)S(1)}, u32[]{:S(2)}) copy-start(f32[1,256]{1,0:T(1,128)S(1)} %get-tuple-element.686) | copy-start | bytes 3076
  129.7 117.0 %copy-start.34 = (f32[1,2,2,128]{3,1,2,0:T(2,128)}, f32[1,2,2,128]{3,1,2,0:T(2,128)S(1)}, u32[]{:S(2)}) copy-start(f32[1,2,2,128]{3,1,2,0:T(2,128)S(1)} %copy.67) | copy-start | bytes 6148
  131.7 115.7 %copy-start.47 = (f32[2]{0:T(128)}, f32[2]{0:T(128)S(1)}, u32[]{:S(2)}) copy-start(f32[2]{0:T(128)S(1)} %slice_reduce_fusion.3) | copy-start | bytes 28
  135.5 111.8 %copy-start.51 = (f32[8]{0:T(128)}, f32[8]{0:T(128)S(1)}, u32[]{:S(2)}) copy-start(f32[8]{0:T(128)S(1)} %slice_dynamic-update-slice_fusion.1) | copy-start | bytes 100
  135.6 112.7 %copy-start = (bf16[2048,128]{1,0:T(8,128)(2,1)S(1)}, bf16[2048,128]{1,0:T(8,128)(2,1)}, u32[]{:S(2)}) copy-start(bf16[2048,128]{1,0:T(8,128)(2,1)} %param.23) | copy-start | bytes 1572868
  248.8 200.7 %copy-start.12 = (bf16[1,256,64]{1,2,0:T(8,128)(2,1)}, bf16[1,256,64]{1,2,0:T(8,128)(2,1)S(1)}, u32[]{:S(2)}) copy-start(bf16[1,256,64]{1,2,0:T(8,128)(2,1)S(1)} %get-tuple-element.658) | copy-start | bytes 98308
  249.0 17.1 copy-start.7
  249.1 200.4 %collective-permute-start = (bf16[3,128]{0,1:T(8,128)(2,1)S(1)}, bf16[3,128]{0,1:T(8,128)(2,1)S(1)}, u32[]{:S(2)}, u32[]{:S(2)}) collective-permute-start(bf16[3,128]{0,1:T(8,128)(2,1)S(1)} %get-tuple-element.670), channel_id=1, source_target_pairs={{0,64},{64,128},{128,192},{192,256},{256,320},{320,384},{384,448},... | collective-permute-start | bytes 2312 | tf_op jit(solution)/shard_map/ppermute | solution.py:19
  256.2 193.4 %collective-permute-start.1 = (bf16[3,128]{0,1:T(8,128)(2,1)S(1)}, bf16[3,128]{0,1:T(8,128)(2,1)S(1)}, u32[]{:S(2)}, u32[]{:S(2)}) collective-permute-start(bf16[3,128]{0,1:T(8,128)(2,1)S(1)} %get-tuple-element.671), channel_id=1, source_target_pairs={{64,0},{128,64},{192,128},{256,192},{320,256},{384,320},{448,384},... | collective-permute-start | bytes 2312 | tf_op jit(solution)/shard_map/ppermute | solution.py:20
  264.4 188.4 %copy-start.48 = (f32[2]{0:T(128)S(1)}, f32[2]{0:T(128)}, u32[]{:S(2)}) copy-start(f32[2]{0:T(128)} %copy-done.47) | copy-start | bytes 28
  449.5 141.2 %copy-start.28 = (f32[2,256]{1,0:T(2,128)}, f32[2,256]{1,0:T(2,128)S(1)}, u32[]{:S(2)}) copy-start(f32[2,256]{1,0:T(2,128)S(1)} %compare_select_fusion.3) | copy-start | bytes 6148
  449.5 4.1 copy-start.26
  451.0 153.2 %copy-start.8 = (bf16[256,64]{0,1:T(8,128)(2,1)S(1)}, bf16[256,64]{0,1:T(8,128)(2,1)}, u32[]{:S(2)}) copy-start(bf16[256,64]{0,1:T(8,128)(2,1)} %copy-done.7) | copy-start | bytes 98308
  451.0 153.2 %copy-start.13 = (bf16[1,256,64]{1,2,0:T(8,128)(2,1)S(1)}, bf16[1,256,64]{1,2,0:T(8,128)(2,1)}, u32[]{:S(2)}) copy-start(bf16[1,256,64]{1,2,0:T(8,128)(2,1)} %copy-done.12) | copy-start | bytes 98308
  451.2 2.4 copy-start.54
  452.8 0.8 copy-start.30
  452.8 0.8 copy-start.32
  452.8 149.2 %copy-start.16 = (f32[2,256,16]{1,2,0:T(8,128)}, f32[2,256,16]{1,2,0:T(8,128)S(1)}, u32[]{:S(2)}) copy-start(f32[2,256,16]{1,2,0:T(8,128)S(1)} %get-tuple-element.633) | copy-start | bytes 98308
  600.9 8.9 copy-start.19
  600.9 8.9 copy-start.35
  602.9 6.9 copy-start.17
  607.7 5.6 copy-start.50
  607.7 6.3 copy-start.49
  609.8 6.9 copy-start.29
  614.9 5.0 copy-start.31
  614.9 5.0 copy-start.33
  614.9 5.0 copy-start.39
  614.9 5.0 copy-start.40
  614.9 5.0 copy-start.41
  614.9 5.0 copy-start.42
  614.9 5.0 copy-start.44
  614.9 5.0 copy-start.45
  615.0 15.3 copy-start.27
  628.8 6.4 copy-start.20
  628.8 6.4 copy-start.53
  632.2 4.4 copy-start.24
  632.2 4.6 copy-start.4
  632.2 4.6 copy-start.9
  632.2 4.6 copy-start.11
  632.2 4.6 copy-start.14
  632.2 4.6 copy-start.36
  632.2 4.6 copy-start.52
  636.5 2.0 copy-start.10
  636.5 2.0 copy-start.15
  636.5 2.0 copy-start.38
  636.5 2.0 copy-start.55
  636.8 2.0 copy-start.23
  636.8 2.2 copy-start.46
  638.8 4.5 copy-start.5
  642.2 1287.4 %all-reduce.30.cloned.1.call-start = ((), (), s32[]{:S(2)}) async-start(), calls=%async_computation.4 | async-start | bytes 1572864 | tf_op jit(solution)/shard_map/psum | solution.py:199
  647.5 14.8 collective-permute-start.2
  657.9 15.9 collective-permute-start.3
  684.9 1.7 copy-start.1
  686.5 0.7 copy-start.22
  686.5 1247.0 %all-reduce.28.cloned.1.call-start = ((), (), s32[]{:S(2)}) async-start(), calls=%async_computation.1 | async-start | bytes 524288 | tf_op jit(solution)/shard_map/psum | solution.py:203
  687.2 0.7 copy-start.6
  687.2 0.7 copy-start.21
  687.2 0.7 copy-start.37
  (1 other events, 0.7 us)
Sparse Core Ops, SparseCore 0:
  10.2 116.4 all-gather.6
  128.8 114.9 all-gather.4
  642.3 783.5 all-reduce.25
  1429.6 199.0 all-reduce.29
  1631.5 145.4 all-reduce.27
